TPU v7x, 32 devices: a whole 2x2x4 slice. The times are simulated.
32 devices in a mesh: expert: 8 (over z, x), tensor: 4 (over y, core).
Axes of the slice: x: 2, y: 2, z: 4, core: 2. Of those that a mesh axis runs over, the one named last changes fastest.
Arguments:
- hidden_in: bfloat16 [4096, 2048], P('expert'), may hold values from -6 to 6
- doc_ids: int32 [8, 512], P('expert'), may hold values from 0 to 2, never falling along the last dimension, each value on 1 to 384 neighbouring positions
- routes: int32 [4096, 8], P('expert'), may hold values from 0 to 15, all different within a row
- out_grad: bfloat16 [4096, 2048], P('expert'), may hold values from -6 to 6
- norm1_gain: float32 [2048], replicated, may hold values from 0.5 to 1.5
- q_weight: bfloat16 [2048, 2048], P(None, 'tensor'), may hold values from -0.125 to 0.125
- k_weight: bfloat16 [2048, 2048], P(None, 'tensor'), may hold values from -0.125 to 0.125
- v_weight: bfloat16 [2048, 2048], P(None, 'tensor'), may hold values from -0.125 to 0.125
- o_weight: bfloat16 [2048, 2048], P(None, 'tensor'), may hold values from -1.5 to 1.5
- q_gain: float32 [128], replicated, may hold values from 0.5 to 1.5
- k_gain: float32 [128], replicated, may hold values from 0.5 to 1.5
- norm2_gain: float32 [2048], replicated, may hold values from 0.5 to 1.5
- router_weight: bfloat16 [2048, 16], replicated, may hold values from -0.0625 to 0.0625
- gate_weight: bfloat16 [16, 2048, 1024], P('expert', None, 'tensor'), may hold values from -0.125 to 0.125
- up_weight: bfloat16 [16, 2048, 1024], P('expert', None, 'tensor'), may hold values from -0.125 to 0.125
- down_weight: bfloat16 [16, 1024, 2048], P('expert', 'tensor'), may hold values from -0.5 to 0.5
Outputs:
- output: bfloat16 [4096, 2048], P('expert')
- input_grad: float32 [4096, 2048], P('expert')
- norm1_gain_grad: float32 [2048], P('expert')
- q_weight_grad: float32 [2048, 2048], P('expert', 'tensor')
- k_weight_grad: float32 [2048, 2048], P('expert', 'tensor')
- v_weight_grad: float32 [2048, 2048], P('expert', 'tensor')
- o_weight_grad: float32 [2048, 2048], P('expert', 'tensor')
- q_gain_grad: float32 [128], P('expert')
- k_gain_grad: float32 [128], P('expert')
- norm2_gain_grad: float32 [2048], P('expert')
- router_weight_grad: float32 [2048, 16], P('expert')
- gate_weight_grad: float32 [16, 2048, 1024], P('expert', None, 'tensor')
- up_weight_grad: float32 [16, 2048, 1024], P('expert', None, 'tensor')
- down_weight_grad: float32 [16, 1024, 2048], P('expert', 'tensor')
Inputs may be any that keep to these rules, and one draw needn't show every extreme that they name: Each row of routes names 8 different experts. `doc_ids`: within a packed row ids never fall; a document has at most 384 tokens.
All inputs are finite; a program needn't handle non-finite values.
Results may differ from a plain program's by a relative error of at most 0.024.
Values may be sent and summed in bfloat16 or wider, within the bound.
No kernel may reach another device: no remote copies, remote signals or barrier semaphores. Data moves between devices by JAX's collectives and lax.ppermute only.
A program may use at most 320 MiB of HBM per device.

v0:
```python
import jax
import jax.numpy as jnp
from jax import lax
from jax.sharding import PartitionSpec as P

epsilon = 1e-06
rope_base = 10000.0
masked_score = -1e30


def rms_scale(values):
    return lax.rsqrt(jnp.mean(values * values, axis=-1, keepdims=True) + epsilon)


def rotary(positions, head_size):
    half_size = head_size // 2
    freqs = rope_base ** (-2.0 * jnp.arange(half_size, dtype=jnp.float32) / head_size)
    angles = jnp.arange(positions, dtype=jnp.float32)[:, None] * freqs[None, :]
    cosine = jnp.cos(angles)
    sine = jnp.sin(angles)
    return (jnp.concatenate([cosine, cosine], -1), jnp.concatenate([sine, sine], -1))


def prep_heads(raw, gain, factor, cosine, sine, heads):
    shaped = raw.reshape(raw.shape[0], heads, -1)
    normed = shaped * rms_scale(shaped) * gain
    half_size = normed.shape[-1] // 2
    turned = jnp.concatenate([-normed[..., half_size:], normed[..., :half_size]], -1)
    return (normed * cosine[:, None, :] + turned * sine[:, None, :]) * factor


def slot_tables(route_rows, all_experts, capacity):
    num_tokens, num_picks = route_rows.shape
    flat_routes = route_rows.reshape(-1)
    onehot = (flat_routes[:, None] == jnp.arange(all_experts, dtype=jnp.int32)[None, :]).astype(
        jnp.int32
    )
    before = jnp.cumsum(onehot, axis=0) - onehot
    placed = jnp.sum(before * onehot, axis=1)
    slot_ids = jnp.where(placed < capacity, flat_routes * capacity + placed, all_experts * capacity)
    pair_ids = jnp.arange(num_tokens * num_picks, dtype=jnp.int32)
    pair_of = (
        jnp.full((all_experts * capacity + 1,), num_tokens * num_picks, jnp.int32)
        .at[slot_ids]
        .set(pair_ids)
    )
    return (slot_ids.reshape(num_tokens, num_picks), pair_of[:-1])


def on_device(
    hidden_in,
    doc_ids,
    routes,
    out_grad,
    norm1_gain,
    q_weight,
    k_weight,
    v_weight,
    o_weight,
    q_gain,
    k_gain,
    norm2_gain,
    router_weight,
    gate_weight,
    up_weight,
    down_weight,
):
    num_tokens, model_width = hidden_in.shape
    num_picks = routes.shape[1]
    head_size = q_gain.shape[0]
    local_heads = q_weight.shape[1] // head_size
    local_experts = gate_weight.shape[0]
    ffn_local = gate_weight.shape[2]
    expert_ranks = lax.axis_size("expert")
    tensor_ranks = lax.axis_size("tensor")
    all_experts = local_experts * expert_ranks
    capacity = tensor_ranks * (
        (9 * num_tokens * num_picks + 8 * all_experts * tensor_ranks - 1)
        // (8 * all_experts * tensor_ranks)
    )
    doc_row = doc_ids[0]
    cosine, sine = rotary(num_tokens, head_size)
    zero_row = jnp.zeros((1, model_width), jnp.bfloat16)
    inputs = hidden_in.astype(jnp.float32)
    scale_one = rms_scale(inputs)
    unit_one = inputs * scale_one
    normed_one = (unit_one * norm1_gain).astype(jnp.bfloat16)
    q_raw = jnp.dot(normed_one, q_weight, preferred_element_type=jnp.float32)
    k_raw = jnp.dot(normed_one, k_weight, preferred_element_type=jnp.float32)
    v_raw = jnp.dot(normed_one, v_weight, preferred_element_type=jnp.float32)

    def shape_heads(q_in, k_in, q_scale, k_scale):
        return (
            prep_heads(q_in, q_scale, head_size ** (-0.5), cosine, sine, local_heads),
            prep_heads(k_in, k_scale, 1.0, cosine, sine, local_heads),
        )

    head_vals, head_back = jax.vjp(shape_heads, q_raw, k_raw, q_gain, k_gain)
    queries = head_vals[0].astype(jnp.bfloat16)
    keys = head_vals[1].astype(jnp.bfloat16)
    values = v_raw.astype(jnp.bfloat16).reshape(num_tokens, local_heads, head_size)

    def block_scores():
        scores = jnp.einsum("qhd,khd->hqk", queries, keys, preferred_element_type=jnp.float32)
        return (
            jnp.where((doc_row[:, None] == doc_row[None, :])[None], scores, masked_score),
            queries,
        )

    scores, query_blk = block_scores()
    peak = jnp.max(scores, -1, keepdims=True)
    log_total = peak + jnp.log(jnp.sum(jnp.exp(scores - peak), -1, keepdims=True))
    weights = jnp.exp(scores - log_total).astype(jnp.bfloat16)
    block_outs = jnp.einsum("hqk,khd->qhd", weights, values, preferred_element_type=jnp.float32)
    attn_out = block_outs.reshape(num_tokens, local_heads * head_size).astype(jnp.bfloat16)
    attn_part = lax.dot_general(
        attn_out, o_weight, (((1,), (1,)), ((), ())), preferred_element_type=jnp.float32
    )
    attn_full = lax.psum(attn_part, "tensor")
    after_attn = inputs + attn_full
    scale_two = rms_scale(after_attn)
    unit_two = after_attn * scale_two
    normed_two = (unit_two * norm2_gain).astype(jnp.bfloat16)
    logits = jnp.dot(normed_two, router_weight, preferred_element_type=jnp.float32)
    pick_mask = routes[:, :, None] == jnp.arange(all_experts, dtype=jnp.int32)[None, None, :]
    chosen = jnp.sum(jnp.where(pick_mask, logits[:, None, :], 0.0), -1)
    gates = jax.nn.softmax(chosen, -1)
    slot_ids, pair_of = slot_tables(routes, all_experts, capacity)
    owners = pair_of // num_picks
    padded_rows = jnp.concatenate([normed_two, zero_row], 0)
    send_buf = jnp.take(padded_rows, owners, axis=0).reshape(
        expert_ranks, local_experts, capacity, model_width
    )
    slot_rows = lax.all_to_all(send_buf, "expert", split_axis=0, concat_axis=0, tiled=True)
    gate_up = jnp.concatenate([gate_weight, up_weight], 2)
    joint_pre = jnp.einsum("secd,edf->secf", slot_rows, gate_up, preferred_element_type=jnp.float32)
    gate_pre = joint_pre[..., :ffn_local]
    up_pre = joint_pre[..., ffn_local:]
    silu_gate = jax.nn.silu(gate_pre)
    hidden = (silu_gate * up_pre).astype(jnp.bfloat16)
    partial_out = jnp.einsum(
        "secf,efd->secd", hidden, down_weight, preferred_element_type=jnp.float32
    ).astype(jnp.bfloat16)
    out_grads = out_grad.astype(jnp.float32)
    mixture = jnp.zeros((num_tokens, model_width), jnp.float32)
    gate_dots = []
    returned = lax.all_to_all(
        partial_out, "expert", split_axis=0, concat_axis=0, tiled=True
    ).reshape(all_experts * capacity, model_width)
    returned = jnp.concatenate([returned, zero_row], 0)
    for rank_k in range(num_picks):
        picked = jnp.take(returned, slot_ids[:, rank_k], axis=0)
        mixture = mixture + gates[:, rank_k, None] * picked
        gate_dots.append(jnp.sum(out_grads * picked, -1))
    moe_full = lax.psum(mixture.astype(jnp.bfloat16), "tensor").astype(jnp.float32)
    output = (after_attn + moe_full).astype(jnp.bfloat16)
    dgate_part = jnp.stack(gate_dots, -1)
    padded_gates = jnp.concatenate([gates.reshape(-1), jnp.zeros((1,), jnp.float32)], 0)
    padded_grads = jnp.concatenate([out_grads, jnp.zeros((1, model_width), jnp.float32)], 0)
    slot_gate = jnp.take(padded_gates, pair_of, axis=0)
    grad_buf = (slot_gate[:, None] * jnp.take(padded_grads, owners, axis=0)).astype(jnp.bfloat16)
    grads_in = lax.all_to_all(
        grad_buf.reshape(expert_ranks, local_experts, capacity, model_width),
        "expert",
        split_axis=0,
        concat_axis=0,
        tiled=True,
    )
    dhidden = jnp.einsum(
        "secd,efd->secf", grads_in, down_weight, preferred_element_type=jnp.float32
    )
    down_grad = jnp.einsum("secf,secd->efd", hidden, grads_in, preferred_element_type=jnp.float32)
    sig_gate = jax.nn.sigmoid(gate_pre)
    dgate_pre = dhidden * up_pre * (sig_gate * (1.0 + gate_pre * (1.0 - sig_gate)))
    dup_pre = dhidden * silu_gate
    djoint = jnp.concatenate([dgate_pre, dup_pre], -1).astype(jnp.bfloat16)
    joint_grad = jnp.einsum("secd,secf->edf", slot_rows, djoint, preferred_element_type=jnp.float32)
    gate_grad = joint_grad[..., :ffn_local]
    up_grad = joint_grad[..., ffn_local:]
    dslot_in = jnp.einsum(
        "secf,edf->secd", djoint, gate_up, preferred_element_type=jnp.float32
    ).astype(jnp.bfloat16)
    dnormed_part = jnp.zeros((num_tokens, model_width), jnp.float32)
    came_back = lax.all_to_all(dslot_in, "expert", split_axis=0, concat_axis=0, tiled=True).reshape(
        all_experts * capacity, model_width
    )
    came_back = jnp.concatenate([came_back, zero_row], 0)
    for rank_k in range(num_picks):
        dnormed_part = dnormed_part + jnp.take(came_back, slot_ids[:, rank_k], axis=0)
    dnormed_exp, dgate_all = lax.psum((dnormed_part, dgate_part), "tensor")
    dsel = gates * (dgate_all - jnp.sum(gates * dgate_all, -1, keepdims=True))
    dlogits = jnp.sum(jnp.where(pick_mask, dsel[:, :, None], 0.0), 1).astype(jnp.bfloat16)
    router_grad = lax.dot_general(
        normed_two, dlogits, (((0,), (0,)), ((), ())), preferred_element_type=jnp.float32
    )
    dnormed_two = dnormed_exp + lax.dot_general(
        dlogits, router_weight, (((1,), (1,)), ((), ())), preferred_element_type=jnp.float32
    )
    norm2_grad = jnp.sum(dnormed_two * unit_two, 0)
    weighted_two = dnormed_two * norm2_gain
    dafter = out_grads + scale_two * (
        weighted_two - unit_two * jnp.mean(weighted_two * unit_two, -1, keepdims=True)
    )
    dattn = dafter.astype(jnp.bfloat16)
    o_grad = lax.dot_general(
        dattn, attn_out, (((0,), (0,)), ((), ())), preferred_element_type=jnp.float32
    )
    dattn_out = (
        jnp.dot(dattn, o_weight, preferred_element_type=jnp.float32)
        .astype(jnp.bfloat16)
        .reshape(num_tokens, local_heads, head_size)
    )
    scores, query_blk = block_scores()
    probs = jnp.exp(scores - log_total)
    dprobs = jnp.einsum("qhd,khd->hqk", dattn_out, values, preferred_element_type=jnp.float32)
    dscores = (probs * (dprobs - jnp.sum(probs * dprobs, -1, keepdims=True))).astype(jnp.bfloat16)
    dquery_blocks = jnp.einsum("hqk,khd->qhd", dscores, keys, preferred_element_type=jnp.float32)
    dkey = jnp.einsum("hqk,qhd->khd", dscores, query_blk, preferred_element_type=jnp.float32)
    dvalue = jnp.einsum(
        "hqk,qhd->khd", probs.astype(jnp.bfloat16), dattn_out, preferred_element_type=jnp.float32
    )
    dq_raw, dk_raw, q_gain_part, k_gain_part = head_back((dquery_blocks, dkey))
    dq_low = dq_raw.astype(jnp.bfloat16)
    dk_low = dk_raw.astype(jnp.bfloat16)
    dv_low = dvalue.reshape(num_tokens, local_heads * head_size).astype(jnp.bfloat16)
    contract_rows = (((0,), (0,)), ((), ()))
    contract_cols = (((1,), (1,)), ((), ()))
    q_grad = lax.dot_general(normed_one, dq_low, contract_rows, preferred_element_type=jnp.float32)
    k_grad = lax.dot_general(normed_one, dk_low, contract_rows, preferred_element_type=jnp.float32)
    v_grad = lax.dot_general(normed_one, dv_low, contract_rows, preferred_element_type=jnp.float32)
    dnormed_one = lax.dot_general(
        dq_low, q_weight, contract_cols, preferred_element_type=jnp.float32
    )
    dnormed_one = dnormed_one + lax.dot_general(
        dk_low, k_weight, contract_cols, preferred_element_type=jnp.float32
    )
    dnormed_one = dnormed_one + lax.dot_general(
        dv_low, v_weight, contract_cols, preferred_element_type=jnp.float32
    )
    dnormed_full, q_gain_sum, k_gain_sum = (
        lax.psum(dnormed_one.astype(jnp.bfloat16), "tensor").astype(jnp.float32),
        lax.psum(q_gain_part.astype(jnp.bfloat16), "tensor").astype(jnp.float32),
        lax.psum(k_gain_part.astype(jnp.bfloat16), "tensor").astype(jnp.float32),
    )
    norm1_grad = jnp.sum(dnormed_full * unit_one, 0)
    weighted_one = dnormed_full * norm1_gain
    input_grad = dafter + scale_one * (
        weighted_one - unit_one * jnp.mean(weighted_one * unit_one, -1, keepdims=True)
    )
    reduced = (
        lax.psum_scatter(
            q_grad.astype(jnp.bfloat16), "expert", scatter_dimension=0, tiled=True
        ).astype(jnp.float32),
        lax.psum_scatter(
            k_grad.astype(jnp.bfloat16), "expert", scatter_dimension=0, tiled=True
        ).astype(jnp.float32),
        lax.psum_scatter(
            v_grad.astype(jnp.bfloat16), "expert", scatter_dimension=0, tiled=True
        ).astype(jnp.float32),
        lax.psum_scatter(
            o_grad.astype(jnp.bfloat16), "expert", scatter_dimension=0, tiled=True
        ).astype(jnp.float32),
        lax.psum_scatter(
            router_grad.astype(jnp.bfloat16), "expert", scatter_dimension=0, tiled=True
        ).astype(jnp.float32),
        lax.psum_scatter(
            norm1_grad.astype(jnp.bfloat16), "expert", scatter_dimension=0, tiled=True
        ).astype(jnp.float32),
        lax.psum_scatter(
            norm2_grad.astype(jnp.bfloat16), "expert", scatter_dimension=0, tiled=True
        ).astype(jnp.float32),
        lax.psum_scatter(
            q_gain_sum.astype(jnp.bfloat16), "expert", scatter_dimension=0, tiled=True
        ).astype(jnp.float32),
        lax.psum_scatter(
            k_gain_sum.astype(jnp.bfloat16), "expert", scatter_dimension=0, tiled=True
        ).astype(jnp.float32),
    )
    return (
        output,
        input_grad,
        reduced[5],
        reduced[0],
        reduced[1],
        reduced[2],
        reduced[3],
        reduced[7],
        reduced[8],
        reduced[6],
        reduced[4],
        gate_grad,
        up_grad,
        down_grad,
    )


def solution(mesh):
    return jax.shard_map(
        on_device,
        mesh=mesh,
        in_specs=(
            P("expert", None),
            P("expert", None),
            P("expert", None),
            P("expert", None),
            P(),
            P(None, "tensor"),
            P(None, "tensor"),
            P(None, "tensor"),
            P(None, "tensor"),
            P(),
            P(),
            P(),
            P(),
            P("expert", None, "tensor"),
            P("expert", None, "tensor"),
            P("expert", "tensor", None),
        ),
        out_specs=(
            P("expert", None),
            P("expert", None),
            P("expert"),
            P("expert", "tensor"),
            P("expert", "tensor"),
            P("expert", "tensor"),
            P("expert", "tensor"),
            P("expert"),
            P("expert"),
            P("expert"),
            P("expert", None),
            P("expert", None, "tensor"),
            P("expert", None, "tensor"),
            P("expert", "tensor", None),
        ),
        check_vma=False,
    )
```

profile of v0, /device:TPU:0, one launch (start us, length us, event | category | flops | bytes accessed | tf_op | source)
XLA Modules:
  0.0 2747.8 jit_solution(8802034476952752222)
XLA Ops:
  11.3 3.7 convolution_convert_fusion.6
  25.3 3.3 fusion.95
  29.7 5.0 reduce-window.6
  36.9 15.5 scatter_custom_fusion
  53.3 63.7 %all-reduce.19.cloned.1.call-done = f32[512,2048]{1,0:T(8,128)} async-done(((f32[512,2048]{1,0:T(8,128)}), f32[512,2048]{1,0:T(8,128)}) %all-reduce.19.cloned.1.call-update) | async-done | bytes 4194320 | tf_op jit(solution)/shard_map/psum | solution.py:119
  117.0 3.5 multiply_reduce_fusion.3
  124.1 36.9 %gather_fusion = bf16[4608,2048]{1,0:T(8,128)(2,1)} fusion(bf16[513,2048]{1,0:T(8,128)(2,1)} %concatenate.39, s32[5120]{0:T(1024)S(1)} %get-tuple-element.104), kind=kCustom, calls=%fused_computation.16 | custom fusion | bytes 37767168 | tf_op jit(solution)/shard_map/jit(_take)/gather | solution.py:131
  161.0 9.7 broadcast_select_fusion
  170.8 413.4 %all_to_all.20 = bf16[8,2,288,2048]{3,2,1,0:T(8,128)(2,1)} all-to-all(bf16[8,2,288,2048]{3,2,1,0:T(8,128)(2,1)S(1)} %broadcast_select_fusion), channel_id=1, replica_groups=mesh['expert'=8,'tensor'=4] {'expert'}, dimensions={0} | all-to-all | bytes 37748736 | tf_op jit(solution)/shard_map/all_to_all | solution.py:134
  584.2 16.5 fusion.42
  600.7 4.5 multiply_convert_fusion.1
  605.2 9.1 convert_bitcast_fusion.1
  614.3 16.9 copy.110
  631.2 5.9 all-to-all-start.1
  637.1 4.1 concatenate.42
  641.3 36.4 %gather_fusion.2 = f32[4608,2048]{1,0:T(8,128)} fusion(f32[513,2048]{1,0:T(8,128)} %concatenate.42, s32[5120]{0:T(1024)S(1)} %get-tuple-element.104), kind=kCustom, calls=%fused_computation.18 | custom fusion | bytes 75515904 | tf_op jit(solution)/shard_map/jit(_take)/gather | solution.py:161
  681.5 362.4 %all-to-all-done.1 = bf16[8,2,288,2048]{3,2,1,0:T(8,128)(2,1)} async-done(((bf16[8,2,288,2048]{3,2,1,0:T(8,128)(2,1)}), bf16[8,2,288,2048]{3,2,1,0:T(8,128)(2,1)}, u32[]{:S(2)}, u32[]{:S(2)}) %all-to-all-start.1) | async-done | bytes 18874400 | tf_op jit(solution)/shard_map/all_to_all | solution.py:147
  1044.0 16.9 concatenate.40
  1060.9 14.0 gather_fusion.10
  1074.9 14.2 gather_fusion.9
  1089.1 14.0 gather_fusion.8
  1103.2 14.4 gather_fusion.7
  1117.6 14.1 gather_fusion.6
  1131.7 14.1 gather_fusion.5
  1145.8 14.2 gather_fusion.4
  1160.0 14.0 gather_fusion.3
  1174.1 8.9 fusion.41
  1183.1 10.1 psum.52
  1194.1 24.1 gather_fusion.1
  1218.4 14.2 multiply_convert_fusion
  1232.6 412.0 %all_to_all.21 = bf16[8,2,288,2048]{3,2,1,0:T(8,128)(2,1)} all-to-all(bf16[8,2,288,2048]{3,2,1,0:T(8,128)(2,1)S(1)} %multiply_convert_fusion), channel_id=1, replica_groups=mesh['expert'=8,'tensor'=4] {'expert'}, dimensions={0} | all-to-all | bytes 37748736 | tf_op jit(solution)/shard_map/all_to_all | solution.py:162
  1644.6 14.0 fusion.12
  1658.6 15.6 convert_bitcast_fusion
  1674.2 9.3 copy.113
  1683.5 411.1 %all_to_all.22 = bf16[8,2,288,2048]{3,2,1,0:T(8,128)(2,1)S(1)} all-to-all(bf16[8,2,288,2048]{3,2,1,0:T(8,128)(2,1)S(1)} %copy.113), channel_id=1, replica_groups=mesh['expert'=8,'tensor'=4] {'expert'}, dimensions={0} | all-to-all | bytes 37748736 | tf_op jit(solution)/shard_map/all_to_all | solution.py:184
  2094.6 8.1 concatenate.44
  2102.7 13.2 gather_fusion.18
  2115.9 14.3 gather_fusion.17
  2130.2 14.0 gather_fusion.16
  2144.2 14.1 gather_fusion.15
  2158.3 14.3 gather_fusion.14
  2172.6 14.1 gather_fusion.13
  2186.7 14.4 gather_fusion.12
  2201.2 14.1 gather_fusion.11
  2215.3 8.4 convert_add_fusion.2
  2226.5 10.0 fusion.29
  2236.6 70.6 %all-reduce.21.cloned.1.call-done = f32[512,2048]{1,0:T(8,128)} async-done(((f32[512,2048]{1,0:T(8,128)}), f32[512,2048]{1,0:T(8,128)}) %all-reduce.21.cloned.1.call-update) | async-done | bytes 4194320 | tf_op jit(solution)/shard_map/psum | solution.py:190
  2307.2 4.9 multiply_reduce_fusion
  2333.0 4.9 convolution_convert_fusion
  2338.0 3.9 convolution_convert_fusion.1
  2343.9 21.3 reduce-scatter.14.cloned.1.call-done
  2369.4 17.9 fusion.17
  2390.2 11.3 fusion.45
  2401.5 51.8 %all-reduce.23.cloned.1.call-done = (bf16[512,2048]{1,0:T(8,128)(2,1)}, bf16[512,2048]{1,0:T(8,128)(2,1)}) async-done(((bf16[512,2048]{1,0:T(8,128)(2,1)}, bf16[512,2048]{1,0:T(8,128)(2,1)}), (bf16[512,2048]{1,0:T(8,128)(2,1)}, bf16[512,2048]{1,0:T(8,128)(2,1)})) %all-reduce.23.cloned.1.call-update) | async-done | bytes 4194320 | tf_op jit(solution)/shard_map/psum | solution.py:155
  2453.3 2.9 fusion.32
  2456.2 22.2 all-reduce.12
  2478.5 7.6 fusion.91
  2486.1 6.0 all-reduce.13
  2494.4 4.4 add_convert_fusion.1
  2500.0 3.3 fusion.21
  2503.3 22.2 reduce-scatter.12.cloned.1.call-done
  2527.3 69.3 %reduce-scatter.10.cloned.1.call-done = bf16[256,512]{1,0:T(8,128)(2,1)} async-done(((bf16[2048,512]{1,0:T(8,128)(2,1)}), bf16[256,512]{1,0:T(8,128)(2,1)}) %reduce-scatter.10.cloned.1.call-update) | async-done | bytes 262160 | tf_op jit(solution)/shard_map/reduce_scatter | solution.py:257
  2598.4 69.4 %reduce-scatter.6.cloned.1.call-done = bf16[256,512]{1,0:T(8,128)(2,1)} async-done(((bf16[2048,512]{1,0:T(8,128)(2,1)}), bf16[256,512]{1,0:T(8,128)(2,1)}) %reduce-scatter.6.cloned.1.call-update) | async-done | bytes 262160 | tf_op jit(solution)/shard_map/reduce_scatter | solution.py:251
  2669.6 69.2 %reduce-scatter.8.cloned.1.call-done = bf16[256,512]{1,0:T(8,128)(2,1)} async-done(((bf16[2048,512]{1,0:T(8,128)(2,1)}), bf16[256,512]{1,0:T(8,128)(2,1)}) %reduce-scatter.8.cloned.1.call-update) | async-done | bytes 262160 | tf_op jit(solution)/shard_map/reduce_scatter | solution.py:254
  (356 shorter events, 68.3 us)
Async XLA Ops:
  7.2 598.0 %copy-start = (bf16[2,256,2048]{2,1,0:T(8,128)(2,1)S(1)}, bf16[2,256,2048]{2,1,0:T(8,128)(2,1)}, u32[]{:S(2)}) copy-start(bf16[2,256,2048]{2,1,0:T(8,128)(2,1)} %param.33) | copy-start | bytes 6291460
  7.2 109.8 %all-reduce.19.cloned.1.call-start = ((), (), s32[]{:S(2)}) async-start(), calls=%async_computation.9 | async-start | bytes 8388608 | tf_op jit(solution)/shard_map/psum | solution.py:119
  9.5 7.6 copy-start.78
  11.3 11.8 copy-start.21
  15.0 8.0 copy-start.45
  52.6 67.9 %copy-start.52 = (s32[8,2,288]{2,1,0:T(2,128)}, s32[8,2,288]{2,1,0:T(2,128)S(1)}, u32[]{:S(2)}) copy-start(s32[8,2,288]{2,1,0:T(2,128)S(1)} %slice.99) | copy-start | bytes 55300
  53.3 107.7 %copy-start.63 = (pred[8,2,288]{2,1,0:T(4,128)(4,1)}, pred[8,2,288]{2,1,0:T(4,128)(4,1)S(1)}, u32[]{:S(2)}) copy-start(pred[8,2,288]{2,1,0:T(4,128)(4,1)S(1)} %compare_and_fusion) | copy-start | bytes 13828
  53.3 67.2 %copy-start.66 = (f32[2048]{0:T(1024)S(1)}, f32[2048]{0:T(1024)}, u32[]{:S(2)}) copy-start(f32[2048]{0:T(1024)} %param.29) | copy-start | bytes 24580
  605.2 9.1 copy-start.19
  631.2 412.7 %all-to-all-start.1 = ((bf16[8,2,288,2048]{3,2,1,0:T(8,128)(2,1)}), bf16[8,2,288,2048]{3,2,1,0:T(8,128)(2,1)}, u32[]{:S(2)}, u32[]{:S(2)}) async-start(bf16[8,2,288,2048]{3,2,1,0:T(8,128)(2,1)} %copy.110), calls=%async_computation.1 | async-start | bytes 37748736 | tf_op jit(solution)/shard_map/all_to_all | solution.py:147
  637.1 1670.1 %all-reduce.21.cloned.1.call-start = ((), (), s32[]{:S(2)}) async-start(), calls=%async_computation.10 | async-start | bytes 8388608 | tf_op jit(solution)/shard_map/psum | solution.py:190
  641.3 36.4 %copy-start.13 = (s32[512,8]{1,0:T(8,128)S(1)}, s32[512,8]{1,0:T(8,128)}, u32[]{:S(2)}) copy-start(s32[512,8]{1,0:T(8,128)} %get-tuple-element.67) | copy-start | bytes 49156
  641.3 37.9 %copy-start.48 = (bf16[2048,16]{0,1:T(8,128)(2,1)S(1)}, bf16[2048,16]{0,1:T(8,128)(2,1)}, u32[]{:S(2)}) copy-start(bf16[2048,16]{0,1:T(8,128)(2,1)} %param.30) | copy-start | bytes 196612
  678.8 467.0 %copy-start.80 = (s32[1024]{0:T(1024)}, s32[1024]{0:T(1024)S(1)}, u32[]{:S(2)}) copy-start(s32[1024]{0:T(1024)S(1)} %pad_clamp_fusion.8) | copy-start | bytes 12292
  678.8 438.8 %copy-start.82 = (s32[1024]{0:T(1024)}, s32[1024]{0:T(1024)S(1)}, u32[]{:S(2)}) copy-start(s32[1024]{0:T(1024)S(1)} %pad_clamp_fusion.6) | copy-start | bytes 12292
  678.9 410.3 %copy-start.86 = (s32[1024]{0:T(1024)}, s32[1024]{0:T(1024)S(1)}, u32[]{:S(2)}) copy-start(s32[1024]{0:T(1024)S(1)} %pad_clamp_fusion.4) | copy-start | bytes 12292
  678.9 382.0 %copy-start.90 = (s32[1024]{0:T(1024)}, s32[1024]{0:T(1024)S(1)}, u32[]{:S(2)}) copy-start(s32[1024]{0:T(1024)S(1)} %pad_clamp_fusion.2) | copy-start | bytes 12292
  678.9 481.1 %copy-start.84 = (s32[1024]{0:T(1024)}, s32[1024]{0:T(1024)S(1)}, u32[]{:S(2)}) copy-start(s32[1024]{0:T(1024)S(1)} %pad_clamp_fusion.9) | copy-start | bytes 12292
  678.9 452.8 %copy-start.88 = (s32[1024]{0:T(1024)}, s32[1024]{0:T(1024)S(1)}, u32[]{:S(2)}) copy-start(s32[1024]{0:T(1024)S(1)} %pad_clamp_fusion.7) | copy-start | bytes 12292
  679.0 424.2 %copy-start.92 = (s32[1024]{0:T(1024)}, s32[1024]{0:T(1024)S(1)}, u32[]{:S(2)}) copy-start(s32[1024]{0:T(1024)S(1)} %pad_clamp_fusion.5) | copy-start | bytes 12292
  679.0 395.9 %copy-start.94 = (s32[1024]{0:T(1024)}, s32[1024]{0:T(1024)S(1)}, u32[]{:S(2)}) copy-start(s32[1024]{0:T(1024)S(1)} %pad_clamp_fusion.3) | copy-start | bytes 12292
  679.0 495.0 %copy-start.96 = (pred[512]{0:T(512)(128)(4,1)}, pred[512]{0:T(512)(128)(4,1)S(1)}, u32[]{:S(2)}) copy-start(pred[512]{0:T(512)(128)(4,1)S(1)} %get-tuple-element.113) | copy-start | bytes 1540
  679.0 495.0 %copy-start.98 = (pred[512]{0:T(512)(128)(4,1)}, pred[512]{0:T(512)(128)(4,1)S(1)}, u32[]{:S(2)}) copy-start(pred[512]{0:T(512)(128)(4,1)S(1)} %get-tuple-element.114) | copy-start | bytes 1540
  679.1 495.0 %copy-start.100 = (pred[512]{0:T(512)(128)(4,1)}, pred[512]{0:T(512)(128)(4,1)S(1)}, u32[]{:S(2)}) copy-start(pred[512]{0:T(512)(128)(4,1)S(1)} %get-tuple-element.115) | copy-start | bytes 1540
  679.1 495.0 %copy-start.102 = (pred[512]{0:T(512)(128)(4,1)}, pred[512]{0:T(512)(128)(4,1)S(1)}, u32[]{:S(2)}) copy-start(pred[512]{0:T(512)(128)(4,1)S(1)} %get-tuple-element.116) | copy-start | bytes 1540
  679.1 495.0 %copy-start.104 = (pred[512]{0:T(512)(128)(4,1)}, pred[512]{0:T(512)(128)(4,1)S(1)}, u32[]{:S(2)}) copy-start(pred[512]{0:T(512)(128)(4,1)S(1)} %get-tuple-element.117) | copy-start | bytes 1540
  679.1 495.0 %copy-start.106 = (pred[512]{0:T(512)(128)(4,1)}, pred[512]{0:T(512)(128)(4,1)S(1)}, u32[]{:S(2)}) copy-start(pred[512]{0:T(512)(128)(4,1)S(1)} %get-tuple-element.118) | copy-start | bytes 1540
  679.1 495.0 %copy-start.108 = (pred[512]{0:T(512)(128)(4,1)}, pred[512]{0:T(512)(128)(4,1)S(1)}, u32[]{:S(2)}) copy-start(pred[512]{0:T(512)(128)(4,1)S(1)} %get-tuple-element.119) | copy-start | bytes 1540
  679.2 495.0 %copy-start.110 = (pred[512]{0:T(512)(128)(4,1)}, pred[512]{0:T(512)(128)(4,1)S(1)}, u32[]{:S(2)}) copy-start(pred[512]{0:T(512)(128)(4,1)S(1)} %get-tuple-element.120) | copy-start | bytes 1540
  1174.1 20.0 copy-start.65
  1193.8 24.4 copy-start.50
  1194.1 24.2 copy-start.53
  1194.1 24.3 copy-start.64
  2094.6 8.1 copy-start.91
  2102.7 13.2 copy-start.95
  2115.9 14.3 copy-start.87
  2130.2 14.0 copy-start.93
  2144.2 14.1 copy-start.83
  2158.3 14.3 copy-start.89
  2172.6 14.1 copy-start.81
  2186.7 14.4 copy-start.85
  2201.1 14.1 copy-start.97
  2201.1 14.1 copy-start.99
  2201.1 14.1 copy-start.101
  2201.1 14.1 copy-start.103
  2201.1 14.1 copy-start.105
  2201.1 14.1 copy-start.107
  2201.2 14.1 copy-start.109
  2201.2 14.1 copy-start.111
  2223.8 141.4 %reduce-scatter.14.cloned.1.call-start = ((), (), s32[]{:S(2)}) async-start(), calls=%async_computation.15 | async-start | bytes 73728 | tf_op jit(solution)/shard_map/reduce_scatter | solution.py:263
  2226.4 226.9 %all-reduce.23.cloned.1.call-start = ((), (), s32[]{:S(2)}) async-start(), calls=%async_computation.16 | async-start | bytes 8388608 | tf_op jit(solution)/shard_map/psum | solution.py:155
  2226.5 80.7 %copy-start.49 = (bf16[2048,16]{0,1:T(8,128)(2,1)S(1)}, bf16[2048,16]{0,1:T(8,128)(2,1)}, u32[]{:S(2)}) copy-start(bf16[2048,16]{0,1:T(8,128)(2,1)} %param.30) | copy-start | bytes 196612
  2226.5 80.7 %copy-start.67 = (f32[2048]{0:T(1024)S(1)}, f32[2048]{0:T(1024)}, u32[]{:S(2)}) copy-start(f32[2048]{0:T(1024)} %param.29) | copy-start | bytes 24580
  2226.5 80.7 %copy-start.77 = (f32[512]{0:T(512)S(1)}, f32[512]{0:T(512)}, u32[]{:S(2)}) copy-start(f32[512]{0:T(512)} %copy-done.76) | copy-start | bytes 6148
  2236.5 75.5 %copy-start.14 = (bf16[512,2048]{1,0:T(8,128)(2,1)S(1)}, bf16[512,2048]{1,0:T(8,128)(2,1)}, u32[]{:S(2)}) copy-start(bf16[512,2048]{1,0:T(8,128)(2,1)} %param.21) | copy-start | bytes 6291460
  2318.7 10.4 copy-start.47
  2332.0 6.0 copy-start.11
  2332.0 193.5 %reduce-scatter.12.cloned.1.call-start = ((), (), s32[]{:S(2)}) async-start(), calls=%async_computation.14 | async-start | bytes 2359296 | tf_op jit(solution)/shard_map/reduce_scatter | solution.py:260
  2337.9 28.6 %copy-start.30 = (bf16[512,4,128]{0,2,1:T(8,128)(2,1)S(1)}, bf16[512,4,128]{0,2,1:T(8,128)(2,1)}, u32[]{:S(2)}) copy-start(bf16[512,4,128]{0,2,1:T(8,128)(2,1)} %copy-done.29) | copy-start | bytes 1572868
  2337.9 258.7 %reduce-scatter.10.cloned.1.call-start = ((), (), s32[]{:S(2)}) async-start(), calls=%async_computation.13 | async-start | bytes 2359296 | tf_op jit(solution)/shard_map/reduce_scatter | solution.py:257
  2342.0 325.8 %reduce-scatter.6.cloned.1.call-start = ((), (), s32[]{:S(2)}) async-start(), calls=%async_computation.11 | async-start | bytes 2359296 | tf_op jit(solution)/shard_map/reduce_scatter | solution.py:251
  2369.4 369.4 %reduce-scatter.8.cloned.1.call-start = ((), (), s32[]{:S(2)}) async-start(), calls=%async_computation.12 | async-start | bytes 2359296 | tf_op jit(solution)/shard_map/reduce_scatter | solution.py:254
  2478.5 15.9 copy-start.42
  2500.0 240.6 %copy-start.1 = (bf16[2,256,2048]{2,1,0:T(8,128)(2,1)S(1)}, bf16[2,256,2048]{2,1,0:T(8,128)(2,1)}, u32[]{:S(2)}) copy-start(bf16[2,256,2048]{2,1,0:T(8,128)(2,1)} %param.33) | copy-start | bytes 6291460
  (63 other events, 141.9 us)
Sparse Core Ops, SparseCore 0:
  28.8 88.1 all-reduce.18
  2223.9 83.1 all-reduce.20
  2310.3 54.8 reduce-scatter.13
  2368.7 84.5 all-reduce.22
  2456.7 68.7 reduce-scatter.11
  2528.9 67.6 reduce-scatter.9
  2600.1 67.6 reduce-scatter.5
  2671.3 67.3 reduce-scatter.7
where the time goes:
time: 2760 us; the launch traced here: 2750 us
  blocking collectives  1270 us (46%)
  waiting for transfers between devices  800 us (29%)
  local copies, waits for them, and re-layouts  420 us (15%)
  matrix products  130 us (5%)
  other arithmetic  99.7 us (4%)
    all_to_all x1, blocking collectives, on_device(): lax.all_to_all(send_buf, 'expert', split_axis=0, concat_axis=0, tiled=True)  413 us
    all_to_all x1, blocking collectives, on_device(): lax.all_to_all(grad_buf.reshape(expert_ranks, local_experts, capacity, mo...  412 us
    all_to_all x1, blocking collectives, on_device(): lax.all_to_all(dslot_in, 'expert', split_axis=0, concat_axis=0, tiled=True)  411 us
    all_to_all x1, waiting for transfers between devices, on_device(): lax.all_to_all(partial_out, 'expert', split_axis=0, concat_axis=0, tiled=...  362 us
    gather x8, local copies, waits for them, and re-layouts, on_device(): picked = jnp.take(returned, slot_ids[:, rank_k], axis=0)  113 us
    gather x8, local copies, waits for them, and re-layouts, on_device(): jnp.take(came_back, slot_ids[:, rank_k], axis=0)  112 us
    psum x1, waiting for transfers between devices, on_device(): dnormed_exp, dgate_all = lax.psum((dnormed_part, dgate_part), 'tensor')  70.6 us
    reduce_scatter x1, waiting for transfers between devices, on_device(): lax.psum_scatter(q_grad.astype(jnp.bfloat16), 'expert', scatter_dimension...  69.4 us
  transfers between devices with their start and end apart: 9, of which 9 were waited for; matrix products, arithmetic and copies ran while one was open for 6% of the time, Pallas kernels for 0%

commit v1 on v0

--- a/solution.py
+++ b/solution.py
@@ -6,6 +6,28 @@
 epsilon = 1e-06
 rope_base = 10000.0
 masked_score = -1e30
+
+
+def in_blocks(value, dim, peers):
+    before, after = (value.shape[:dim], value.shape[dim + 1 :])
+    return jnp.moveaxis(value.reshape(*before, peers, -1, *after), dim, 0)
+
+
+def joined_along(pieces, dim):
+    lengths = list(pieces.shape[1:])
+    lengths[dim] *= pieces.shape[0]
+    return jnp.moveaxis(pieces, 0, dim).reshape(lengths)
+
+
+def pairwise_exchange(value, axis, split_dim, concat_dim):
+    length, index = (lax.axis_size(axis), lax.axis_index(axis))
+    tiles = in_blocks(value, split_dim, length)
+    outs = [tiles[index]]
+    for turn in range(1, length):
+        sent = tiles[index ^ turn]
+        outs.append(lax.ppermute(sent, axis, [(i, i ^ turn) for i in range(length)]))
+    tiles = jnp.stack(outs)[index ^ jnp.arange(length)]
+    return joined_along(tiles, concat_dim)
 
 
 def rms_scale(values):
@@ -181,7 +203,7 @@
         "secf,edf->secd", djoint, gate_up, preferred_element_type=jnp.float32
     ).astype(jnp.bfloat16)
     dnormed_part = jnp.zeros((num_tokens, model_width), jnp.float32)
-    came_back = lax.all_to_all(dslot_in, "expert", split_axis=0, concat_axis=0, tiled=True).reshape(
+    came_back = pairwise_exchange(dslot_in, "expert", 0, 0).reshape(
         all_experts * capacity, model_width
     )
     came_back = jnp.concatenate([came_back, zero_row], 0)

time: 2760 us -> 2800 us (1.014)
  blocking collectives: 1270 us -> 452 us
  waiting for transfers between devices: 800 us -> 1600 us
  local copies, waits for them, and re-layouts: 420 us -> 457 us
    all_to_all x2 -> x0, blocking collectives: 823 us -> none  [the longest x1 412 us: on_device(): lax.all_to_all(grad_buf.reshape(expert_ranks, local_experts, capacity, mo...]
    all_to_all x0 -> x1, waiting for transfers between devices: none -> 406 us  [on_device(): lax.all_to_all(grad_buf.reshape(expert_ranks, local_experts, capacity, mo...]
    ppermute x0 -> x7, waiting for transfers between devices: none -> 291 us  [pairwise_exchange(): lax.ppermute(sent, axis, [(i, i ^ turn) for i in range(length)])]
    psum x1, waiting for transfers between devices: 70.6 us -> 170 us  [on_device(): dnormed_exp, dgate_all = lax.psum((dnormed_part, dgate_part), 'tensor')]
  transfers between devices with their start and end apart: 9 -> 17, of which waited for: 9 -> 14; matrix products, arithmetic and copies ran while one was open for 6% -> 6% of each run, Pallas kernels for 0% -> 0%
where the time goes in v1:
time: 2800 us; the launch traced here: 2790 us
  waiting for transfers between devices  1600 us (57%)
  local copies, waits for them, and re-layouts  457 us (16%)
  blocking collectives  452 us (16%)
  matrix products  130 us (5%)
  other arithmetic  116 us (4%)
    all_to_all x1, blocking collectives, on_device(): lax.all_to_all(send_buf, 'expert', split_axis=0, concat_axis=0, tiled=True)  413 us
    all_to_all x1, waiting for transfers between devices, on_device(): lax.all_to_all(grad_buf.reshape(expert_ranks, local_experts, capacity, mo...  406 us
    all_to_all x1, waiting for transfers between devices, on_device(): lax.all_to_all(partial_out, 'expert', split_axis=0, concat_axis=0, tiled=...  363 us
    ppermute x7, waiting for transfers between devices, pairwise_exchange(): lax.ppermute(sent, axis, [(i, i ^ turn) for i in range(length)])  291 us
    psum x1, waiting for transfers between devices, on_device(): dnormed_exp, dgate_all = lax.psum((dnormed_part, dgate_part), 'tensor')  170 us
    gather x8, local copies, waits for them, and re-layouts, on_device(): picked = jnp.take(returned, slot_ids[:, rank_k], axis=0)  113 us
    gather x8, local copies, waits for them, and re-layouts, on_device(): jnp.take(came_back, slot_ids[:, rank_k], axis=0)  112 us
    reduce_scatter x1, waiting for transfers between devices, on_device(): lax.psum_scatter(q_grad.astype(jnp.bfloat16), 'expert', scatter_dimension...  69.4 us
  transfers between devices with their start and end apart: 17, of which 14 were waited for; matrix products, arithmetic and copies ran while one was open for 6% of the time, Pallas kernels for 0%

profile of v1, /device:TPU:0, one launch (start us, length us, event | category | flops | bytes accessed | tf_op | source)
XLA Modules:
  0.0 2794.2 jit_solution(17151156353194940265)
XLA Ops:
  29.7 4.8 reduce-window.6
  36.8 15.5 scatter_custom_fusion
  53.2 63.9 %all-reduce.19.cloned.1.call-done = f32[512,2048]{1,0:T(8,128)} async-done(((f32[512,2048]{1,0:T(8,128)}), f32[512,2048]{1,0:T(8,128)}) %all-reduce.19.cloned.1.call-update) | async-done | bytes 4194320 | tf_op jit(solution)/shard_map/psum | solution.py:141
  124.2 36.9 %gather_fusion = bf16[4608,2048]{1,0:T(8,128)(2,1)} fusion(bf16[513,2048]{1,0:T(8,128)(2,1)} %concatenate.39, s32[5120]{0:T(1024)S(1)} %get-tuple-element.129), kind=kCustom, calls=%fused_computation.16 | custom fusion | bytes 37767168 | tf_op jit(solution)/shard_map/jit(_take)/gather | solution.py:153
  161.1 9.7 broadcast_select_fusion
  170.9 413.4 %all_to_all.15 = bf16[8,2,288,2048]{3,2,1,0:T(8,128)(2,1)} all-to-all(bf16[8,2,288,2048]{3,2,1,0:T(8,128)(2,1)S(1)} %broadcast_select_fusion), channel_id=1, replica_groups=mesh['expert'=8,'tensor'=4] {'expert'}, dimensions={0} | all-to-all | bytes 37748736 | tf_op jit(solution)/shard_map/all_to_all | solution.py:156
  584.3 16.5 fusion.42
  600.7 4.5 multiply_convert_fusion.1
  605.2 9.1 convert_bitcast_fusion
  614.3 16.9 copy.135
  631.3 6.1 all-to-all-start.1
  641.5 36.2 %gather_fusion.2 = f32[4608,2048]{1,0:T(8,128)} fusion(f32[513,2048]{1,0:T(8,128)} %concatenate.42, s32[5120]{0:T(1024)S(1)} %get-tuple-element.129), kind=kCustom, calls=%fused_computation.18 | custom fusion | bytes 75515904 | tf_op jit(solution)/shard_map/jit(_take)/gather | solution.py:183
  681.6 362.6 %all-to-all-done.1 = bf16[8,2,288,2048]{3,2,1,0:T(8,128)(2,1)} async-done(((bf16[8,2,288,2048]{3,2,1,0:T(8,128)(2,1)}), bf16[8,2,288,2048]{3,2,1,0:T(8,128)(2,1)}, u32[]{:S(2)}, u32[]{:S(2)}) %all-to-all-start.1) | async-done | bytes 18874400 | tf_op jit(solution)/shard_map/all_to_all | solution.py:169
  1044.2 16.9 concatenate.40
  1061.2 14.0 gather_fusion.12
  1075.2 14.5 gather_fusion.11
  1089.7 14.1 gather_fusion.10
  1103.8 14.2 gather_fusion.9
  1118.0 14.0 gather_fusion.8
  1132.1 14.0 gather_fusion.7
  1146.1 14.2 gather_fusion.6
  1160.3 14.1 gather_fusion.5
  1174.5 8.9 fusion.41
  1183.4 10.1 psum.52
  1194.5 24.1 gather_fusion.1
  1218.8 21.3 multiply_convert_fusion
  1240.1 5.9 all-to-all-start.2
  1246.1 406.4 %all-to-all-done.2 = bf16[8,2,288,2048]{3,2,1,0:T(8,128)(2,1)} async-done(((bf16[8,2,288,2048]{3,2,1,0:T(8,128)(2,1)}), bf16[8,2,288,2048]{3,2,1,0:T(8,128)(2,1)}, u32[]{:S(2)}, u32[]{:S(2)}) %all-to-all-start.2) | async-done | bytes 18874400 | tf_op jit(solution)/shard_map/all_to_all | solution.py:184
  1652.5 14.4 fusion.12
  1666.9 15.8 convolution_convert_fusion
  1682.6 12.0 dynamic-slice_bitcast_fusion
  1704.0 43.1 %collective-permute-done = bf16[1,2,288,2048]{3,2,1,0:T(8,128)(2,1)} collective-permute-done((bf16[1,2,288,2048]{3,2,1,0:T(8,128)(2,1)}, bf16[1,2,288,2048]{3,2,1,0:T(8,128)(2,1)}, u32[]{:S(2)}, u32[]{:S(2)}) %collective-permute-start) | collective-permute-done | bytes 2359328 | tf_op jit(solution)/shard_map/ppermute | solution.py:28
  1752.3 97.2 %collective-permute-done.1 = bf16[1,2,288,2048]{3,2,1,0:T(8,128)(2,1)} collective-permute-done((bf16[1,2,288,2048]{3,2,1,0:T(8,128)(2,1)}, bf16[1,2,288,2048]{3,2,1,0:T(8,128)(2,1)}, u32[]{:S(2)}, u32[]{:S(2)}) %collective-permute-start.1) | collective-permute-done | bytes 2359328 | tf_op jit(solution)/shard_map/ppermute | solution.py:28
  1852.5 45.3 %collective-permute-done.2 = bf16[1,2,288,2048]{3,2,1,0:T(8,128)(2,1)} collective-permute-done((bf16[1,2,288,2048]{3,2,1,0:T(8,128)(2,1)}, bf16[1,2,288,2048]{3,2,1,0:T(8,128)(2,1)}, u32[]{:S(2)}, u32[]{:S(2)}) %collective-permute-start.2) | collective-permute-done | bytes 2359328 | tf_op jit(solution)/shard_map/ppermute | solution.py:28
  1901.4 105.7 %collective-permute-done.4 = bf16[1,2,288,2048]{3,2,1,0:T(8,128)(2,1)S(1)} collective-permute-done((bf16[1,2,288,2048]{3,2,1,0:T(8,128)(2,1)}, bf16[1,2,288,2048]{3,2,1,0:T(8,128)(2,1)S(1)}, u32[]{:S(2)}, u32[]{:S(2)}) %collective-permute-start.4) | collective-permute-done | bytes 2359328 | tf_op jit(solution)/shard_map/ppermute | solution.py:28
  2007.7 6.9 slice_bitcast_fusion.1
  2014.6 8.8 gather_fusion.3
  2023.4 8.9 gather_fusion.4
  2032.3 9.4 pad_maximum_fusion
  2041.6 8.2 concatenate.44
  2049.9 13.2 gather_fusion.20
  2063.1 14.0 gather_fusion.19
  2077.2 14.5 gather_fusion.18
  2091.7 14.1 gather_fusion.17
  2105.7 14.3 gather_fusion.16
  2120.0 14.1 gather_fusion.15
  2134.1 14.1 gather_fusion.14
  2148.2 14.1 gather_fusion.13
  2162.4 8.4 convert_add_fusion.2
  2173.6 9.8 fusion.29
  2183.4 170.3 %all-reduce.21.cloned.1.call-done = f32[512,2048]{1,0:T(8,128)} async-done(((f32[512,2048]{1,0:T(8,128)}), f32[512,2048]{1,0:T(8,128)}) %all-reduce.21.cloned.1.call-update) | async-done | bytes 4194320 | tf_op jit(solution)/shard_map/psum | solution.py:212
  2353.7 4.9 multiply_reduce_fusion
  2379.6 4.8 convolution_convert_fusion.1
  2390.5 21.3 reduce-scatter.14.cloned.1.call-done
  2416.0 18.0 fusion.17
  2436.9 11.3 fusion.45
  2448.1 51.7 %all-reduce.23.cloned.1.call-done = (bf16[512,2048]{1,0:T(8,128)(2,1)}, bf16[512,2048]{1,0:T(8,128)(2,1)}) async-done(((bf16[512,2048]{1,0:T(8,128)(2,1)}, bf16[512,2048]{1,0:T(8,128)(2,1)}), (bf16[512,2048]{1,0:T(8,128)(2,1)}, bf16[512,2048]{1,0:T(8,128)(2,1)})) %all-reduce.23.cloned.1.call-update) | async-done | bytes 4194320 | tf_op jit(solution)/shard_map/psum | solution.py:177
  2502.8 22.2 all-reduce.12
  2525.1 7.6 fusion.92
  2532.7 6.0 all-reduce.13
  2549.9 22.2 reduce-scatter.12.cloned.1.call-done
  2573.9 69.3 %reduce-scatter.10.cloned.1.call-done = bf16[256,512]{1,0:T(8,128)(2,1)} async-done(((bf16[2048,512]{1,0:T(8,128)(2,1)}), bf16[256,512]{1,0:T(8,128)(2,1)}) %reduce-scatter.10.cloned.1.call-update) | async-done | bytes 262160 | tf_op jit(solution)/shard_map/reduce_scatter | solution.py:279
  2645.0 69.4 %reduce-scatter.6.cloned.1.call-done = bf16[256,512]{1,0:T(8,128)(2,1)} async-done(((bf16[2048,512]{1,0:T(8,128)(2,1)}), bf16[256,512]{1,0:T(8,128)(2,1)}) %reduce-scatter.6.cloned.1.call-update) | async-done | bytes 262160 | tf_op jit(solution)/shard_map/reduce_scatter | solution.py:273
  2716.2 69.1 %reduce-scatter.8.cloned.1.call-done = bf16[256,512]{1,0:T(8,128)(2,1)} async-done(((bf16[2048,512]{1,0:T(8,128)(2,1)}), bf16[256,512]{1,0:T(8,128)(2,1)}) %reduce-scatter.8.cloned.1.call-update) | async-done | bytes 262160 | tf_op jit(solution)/shard_map/reduce_scatter | solution.py:276
  (388 shorter events, 119.3 us)
Async XLA Ops:
  7.2 598.1 %copy-start = (bf16[2,256,2048]{2,1,0:T(8,128)(2,1)S(1)}, bf16[2,256,2048]{2,1,0:T(8,128)(2,1)}, u32[]{:S(2)}) copy-start(bf16[2,256,2048]{2,1,0:T(8,128)(2,1)} %param.33) | copy-start | bytes 6291460
  7.2 109.9 %all-reduce.19.cloned.1.call-start = ((), (), s32[]{:S(2)}) async-start(), calls=%async_computation.8 | async-start | bytes 8388608 | tf_op jit(solution)/shard_map/psum | solution.py:141
  52.5 68.1 %copy-start.54 = (s32[8,2,288]{2,1,0:T(2,128)}, s32[8,2,288]{2,1,0:T(2,128)S(1)}, u32[]{:S(2)}) copy-start(s32[8,2,288]{2,1,0:T(2,128)S(1)} %slice.99) | copy-start | bytes 55300
  53.2 107.9 %copy-start.65 = (pred[8,2,288]{2,1,0:T(4,128)(4,1)}, pred[8,2,288]{2,1,0:T(4,128)(4,1)S(1)}, u32[]{:S(2)}) copy-start(pred[8,2,288]{2,1,0:T(4,128)(4,1)S(1)} %compare_and_fusion) | copy-start | bytes 13828
  53.2 67.4 %copy-start.68 = (f32[2048]{0:T(1024)S(1)}, f32[2048]{0:T(1024)}, u32[]{:S(2)}) copy-start(f32[2048]{0:T(1024)} %param.29) | copy-start | bytes 24580
  631.3 413.0 %all-to-all-start.1 = ((bf16[8,2,288,2048]{3,2,1,0:T(8,128)(2,1)}), bf16[8,2,288,2048]{3,2,1,0:T(8,128)(2,1)}, u32[]{:S(2)}, u32[]{:S(2)}) async-start(bf16[8,2,288,2048]{3,2,1,0:T(8,128)(2,1)} %copy.135), calls=%async_computation.1 | async-start | bytes 37748736 | tf_op jit(solution)/shard_map/all_to_all | solution.py:169
  641.5 36.2 %copy-start.13 = (s32[512,8]{1,0:T(8,128)S(1)}, s32[512,8]{1,0:T(8,128)}, u32[]{:S(2)}) copy-start(s32[512,8]{1,0:T(8,128)} %get-tuple-element.76) | copy-start | bytes 49156
  641.5 37.7 %copy-start.50 = (bf16[2048,16]{0,1:T(8,128)(2,1)S(1)}, bf16[2048,16]{0,1:T(8,128)(2,1)}, u32[]{:S(2)}) copy-start(bf16[2048,16]{0,1:T(8,128)(2,1)} %param.30) | copy-start | bytes 196612
  678.9 467.2 %copy-start.82 = (s32[1024]{0:T(1024)}, s32[1024]{0:T(1024)S(1)}, u32[]{:S(2)}) copy-start(s32[1024]{0:T(1024)S(1)} %pad_clamp_fusion.9) | copy-start | bytes 12292
  678.9 439.1 %copy-start.84 = (s32[1024]{0:T(1024)}, s32[1024]{0:T(1024)S(1)}, u32[]{:S(2)}) copy-start(s32[1024]{0:T(1024)S(1)} %pad_clamp_fusion.7) | copy-start | bytes 12292
  678.9 410.8 %copy-start.88 = (s32[1024]{0:T(1024)}, s32[1024]{0:T(1024)S(1)}, u32[]{:S(2)}) copy-start(s32[1024]{0:T(1024)S(1)} %pad_clamp_fusion.5) | copy-start | bytes 12292
  679.0 382.2 %copy-start.92 = (s32[1024]{0:T(1024)}, s32[1024]{0:T(1024)S(1)}, u32[]{:S(2)}) copy-start(s32[1024]{0:T(1024)S(1)} %pad_clamp_fusion.3) | copy-start | bytes 12292
  679.0 481.3 %copy-start.86 = (s32[1024]{0:T(1024)}, s32[1024]{0:T(1024)S(1)}, u32[]{:S(2)}) copy-start(s32[1024]{0:T(1024)S(1)} %pad_clamp_fusion.10) | copy-start | bytes 12292
  679.0 453.0 %copy-start.90 = (s32[1024]{0:T(1024)}, s32[1024]{0:T(1024)S(1)}, u32[]{:S(2)}) copy-start(s32[1024]{0:T(1024)S(1)} %pad_clamp_fusion.8) | copy-start | bytes 12292
  679.0 424.8 %copy-start.94 = (s32[1024]{0:T(1024)}, s32[1024]{0:T(1024)S(1)}, u32[]{:S(2)}) copy-start(s32[1024]{0:T(1024)S(1)} %pad_clamp_fusion.6) | copy-start | bytes 12292
  679.1 396.1 %copy-start.96 = (s32[1024]{0:T(1024)}, s32[1024]{0:T(1024)S(1)}, u32[]{:S(2)}) copy-start(s32[1024]{0:T(1024)S(1)} %pad_clamp_fusion.4) | copy-start | bytes 12292
  679.1 495.3 %copy-start.98 = (pred[512]{0:T(512)(128)(4,1)}, pred[512]{0:T(512)(128)(4,1)S(1)}, u32[]{:S(2)}) copy-start(pred[512]{0:T(512)(128)(4,1)S(1)} %get-tuple-element.120) | copy-start | bytes 1540
  679.1 495.3 %copy-start.100 = (pred[512]{0:T(512)(128)(4,1)}, pred[512]{0:T(512)(128)(4,1)S(1)}, u32[]{:S(2)}) copy-start(pred[512]{0:T(512)(128)(4,1)S(1)} %get-tuple-element.121) | copy-start | bytes 1540
  679.1 495.3 %copy-start.102 = (pred[512]{0:T(512)(128)(4,1)}, pred[512]{0:T(512)(128)(4,1)S(1)}, u32[]{:S(2)}) copy-start(pred[512]{0:T(512)(128)(4,1)S(1)} %get-tuple-element.122) | copy-start | bytes 1540
  679.1 495.3 %copy-start.104 = (pred[512]{0:T(512)(128)(4,1)}, pred[512]{0:T(512)(128)(4,1)S(1)}, u32[]{:S(2)}) copy-start(pred[512]{0:T(512)(128)(4,1)S(1)} %get-tuple-element.123) | copy-start | bytes 1540
  679.2 495.3 %copy-start.106 = (pred[512]{0:T(512)(128)(4,1)}, pred[512]{0:T(512)(128)(4,1)S(1)}, u32[]{:S(2)}) copy-start(pred[512]{0:T(512)(128)(4,1)S(1)} %get-tuple-element.124) | copy-start | bytes 1540
  679.2 495.3 %copy-start.108 = (pred[512]{0:T(512)(128)(4,1)}, pred[512]{0:T(512)(128)(4,1)S(1)}, u32[]{:S(2)}) copy-start(pred[512]{0:T(512)(128)(4,1)S(1)} %get-tuple-element.125) | copy-start | bytes 1540
  679.2 495.2 %copy-start.110 = (pred[512]{0:T(512)(128)(4,1)}, pred[512]{0:T(512)(128)(4,1)S(1)}, u32[]{:S(2)}) copy-start(pred[512]{0:T(512)(128)(4,1)S(1)} %get-tuple-element.126) | copy-start | bytes 1540
  679.2 495.2 %copy-start.112 = (pred[512]{0:T(512)(128)(4,1)}, pred[512]{0:T(512)(128)(4,1)S(1)}, u32[]{:S(2)}) copy-start(pred[512]{0:T(512)(128)(4,1)S(1)} %get-tuple-element.127) | copy-start | bytes 1540
  1174.5 20.0 copy-start.67
  1194.2 24.4 copy-start.52
  1194.5 24.2 copy-start.55
  1194.5 24.3 copy-start.66
  1240.1 412.4 %all-to-all-start.2 = ((bf16[8,2,288,2048]{3,2,1,0:T(8,128)(2,1)}), bf16[8,2,288,2048]{3,2,1,0:T(8,128)(2,1)}, u32[]{:S(2)}, u32[]{:S(2)}) async-start(bf16[8,2,288,2048]{3,2,1,0:T(8,128)(2,1)} %multiply_convert_fusion), calls=%async_computation.2 | async-start | bytes 37748736 | tf_op jit(solution)/shard_map/all_to_all | solution.py:184
  1246.0 1107.7 %all-reduce.21.cloned.1.call-start = ((), (), s32[]{:S(2)}) async-start(), calls=%async_computation.9 | async-start | bytes 8388608 | tf_op jit(solution)/shard_map/psum | solution.py:212
  1694.7 52.4 %collective-permute-start = (bf16[1,2,288,2048]{3,2,1,0:T(8,128)(2,1)}, bf16[1,2,288,2048]{3,2,1,0:T(8,128)(2,1)}, u32[]{:S(2)}, u32[]{:S(2)}) collective-permute-start(bf16[1,2,288,2048]{3,2,1,0:T(8,128)(2,1)} %get-tuple-element.60), channel_id=1, source_target_pairs={{0,4},{4,0},{8,12},{12,8},{16,20},{20,16},{24,28},{28,24},{1,5},{5... | collective-permute-start | bytes 7077896 | tf_op jit(solution)/shard_map/ppermute | solution.py:28
  1696.2 153.4 %collective-permute-start.1 = (bf16[1,2,288,2048]{3,2,1,0:T(8,128)(2,1)}, bf16[1,2,288,2048]{3,2,1,0:T(8,128)(2,1)}, u32[]{:S(2)}, u32[]{:S(2)}) collective-permute-start(bf16[1,2,288,2048]{3,2,1,0:T(8,128)(2,1)} %get-tuple-element.59), channel_id=1, source_target_pairs={{0,8},{4,12},{8,0},{12,4},{16,24},{20,28},{24,16},{28,20},{1,9},{5... | collective-permute-start | bytes 7077896 | tf_op jit(solution)/shard_map/ppermute | solution.py:28
  1696.2 201.5 %collective-permute-start.2 = (bf16[1,2,288,2048]{3,2,1,0:T(8,128)(2,1)}, bf16[1,2,288,2048]{3,2,1,0:T(8,128)(2,1)}, u32[]{:S(2)}, u32[]{:S(2)}) collective-permute-start(bf16[1,2,288,2048]{3,2,1,0:T(8,128)(2,1)} %get-tuple-element.58), channel_id=1, source_target_pairs={{0,12},{4,8},{8,4},{12,0},{16,28},{20,24},{24,20},{28,16},{1,13},{... | collective-permute-start | bytes 7077896 | tf_op jit(solution)/shard_map/ppermute | solution.py:28
  1698.2 201.4 %collective-permute-start.3 = (bf16[1,2,288,2048]{3,2,1,0:T(8,128)(2,1)}, bf16[1,2,288,2048]{3,2,1,0:T(8,128)(2,1)}, u32[]{:S(2)}, u32[]{:S(2)}) collective-permute-start(bf16[1,2,288,2048]{3,2,1,0:T(8,128)(2,1)} %get-tuple-element.57), channel_id=1, source_target_pairs={{0,16},{4,20},{8,24},{12,28},{16,0},{20,4},{24,8},{28,12},{1,17},{... | collective-permute-start | bytes 7077896 | tf_op jit(solution)/shard_map/ppermute | solution.py:28
  1699.0 48.0 %copy-start.36 = (bf16[1,2,288,2048]{3,2,1,0:T(8,128)(2,1)S(1)}, bf16[1,2,288,2048]{3,2,1,0:T(8,128)(2,1)}, u32[]{:S(2)}) copy-start(bf16[1,2,288,2048]{3,2,1,0:T(8,128)(2,1)} %get-tuple-element.61) | copy-start | bytes 7077892
  1699.1 150.5 %copy-start.35 = (bf16[1,2,288,2048]{3,2,0,1:T(8,128)(2,1)S(1)}, bf16[1,2,288,2048]{3,2,0,1:T(8,128)(2,1)}, u32[]{:S(2)}) copy-start(bf16[1,2,288,2048]{3,2,0,1:T(8,128)(2,1)} %get-tuple-element.55) | copy-start | bytes 7077892
  1699.1 308.1 %collective-permute-start.4 = (bf16[1,2,288,2048]{3,2,1,0:T(8,128)(2,1)}, bf16[1,2,288,2048]{3,2,1,0:T(8,128)(2,1)S(1)}, u32[]{:S(2)}, u32[]{:S(2)}) collective-permute-start(bf16[1,2,288,2048]{3,2,1,0:T(8,128)(2,1)} %get-tuple-element.56), channel_id=1, source_target_pairs={{0,20},{4,16},{8,28},{12,24},{16,4},{20,0},{24,12},{28,8},{1,21},{... | collective-permute-start | bytes 7077896 | tf_op jit(solution)/shard_map/ppermute | solution.py:28
  1747.0 260.3 %collective-permute-start.5 = (bf16[1,2,288,2048]{3,2,1,0:T(8,128)(2,1)S(1)}, bf16[1,2,288,2048]{3,2,1,0:T(8,128)(2,1)S(1)}, u32[]{:S(2)}, u32[]{:S(2)}) collective-permute-start(bf16[1,2,288,2048]{3,2,1,0:T(8,128)(2,1)S(1)} %copy-done.36), channel_id=1, source_target_pairs={{0,24},{4,28},{8,16},{12,20},{16,8},{20,12},{24,0},{28,4},{1,25},{... | collective-permute-start | bytes 7077896 | tf_op jit(solution)/shard_map/ppermute | solution.py:28
  1849.6 157.9 %collective-permute-start.6 = (bf16[1,2,288,2048]{3,2,0,1:T(8,128)(2,1)S(1)}, bf16[1,2,288,2048]{3,2,0,1:T(8,128)(2,1)S(1)}, u32[]{:S(2)}, u32[]{:S(2)}) collective-permute-start(bf16[1,2,288,2048]{3,2,0,1:T(8,128)(2,1)S(1)} %copy-done.35), channel_id=1, source_target_pairs={{0,28},{4,24},{8,20},{12,16},{16,12},{20,8},{24,4},{28,0},{1,29},{... | collective-permute-start | bytes 7077896 | tf_op jit(solution)/shard_map/ppermute | solution.py:28
  2077.2 14.5 copy-start.95
  2091.7 14.1 copy-start.85
  2105.7 14.3 copy-start.91
  2120.0 14.1 copy-start.83
  2148.1 14.2 copy-start.99
  2148.1 14.2 copy-start.101
  2148.2 14.2 copy-start.103
  2148.2 14.2 copy-start.105
  2148.2 14.2 copy-start.107
  2148.2 14.2 copy-start.109
  2148.2 14.2 copy-start.111
  2148.2 14.2 copy-start.113
  2170.9 240.9 %reduce-scatter.14.cloned.1.call-start = ((), (), s32[]{:S(2)}) async-start(), calls=%async_computation.14 | async-start | bytes 73728 | tf_op jit(solution)/shard_map/reduce_scatter | solution.py:285
  2173.5 326.4 %all-reduce.23.cloned.1.call-start = ((), (), s32[]{:S(2)}) async-start(), calls=%async_computation.15 | async-start | bytes 8388608 | tf_op jit(solution)/shard_map/psum | solution.py:177
  2173.6 180.2 %copy-start.51 = (bf16[2048,16]{0,1:T(8,128)(2,1)S(1)}, bf16[2048,16]{0,1:T(8,128)(2,1)}, u32[]{:S(2)}) copy-start(bf16[2048,16]{0,1:T(8,128)(2,1)} %param.30) | copy-start | bytes 196612
  2173.6 180.2 %copy-start.69 = (f32[2048]{0:T(1024)S(1)}, f32[2048]{0:T(1024)}, u32[]{:S(2)}) copy-start(f32[2048]{0:T(1024)} %param.29) | copy-start | bytes 24580
  2173.6 180.2 %copy-start.79 = (f32[512]{0:T(512)S(1)}, f32[512]{0:T(512)}, u32[]{:S(2)}) copy-start(f32[512]{0:T(512)} %copy-done.78) | copy-start | bytes 6148
  2183.4 175.3 %copy-start.14 = (bf16[512,2048]{1,0:T(8,128)(2,1)S(1)}, bf16[512,2048]{1,0:T(8,128)(2,1)}, u32[]{:S(2)}) copy-start(bf16[512,2048]{1,0:T(8,128)(2,1)} %param.21) | copy-start | bytes 6291460
  2378.6 193.5 %reduce-scatter.12.cloned.1.call-start = ((), (), s32[]{:S(2)}) async-start(), calls=%async_computation.13 | async-start | bytes 2359296 | tf_op jit(solution)/shard_map/reduce_scatter | solution.py:282
  2384.5 28.6 %copy-start.30 = (bf16[512,4,128]{0,2,1:T(8,128)(2,1)S(1)}, bf16[512,4,128]{0,2,1:T(8,128)(2,1)}, u32[]{:S(2)}) copy-start(bf16[512,4,128]{0,2,1:T(8,128)(2,1)} %copy-done.29) | copy-start | bytes 1572868
  2384.5 258.7 %reduce-scatter.10.cloned.1.call-start = ((), (), s32[]{:S(2)}) async-start(), calls=%async_computation.12 | async-start | bytes 2359296 | tf_op jit(solution)/shard_map/reduce_scatter | solution.py:279
  2388.6 325.8 %reduce-scatter.6.cloned.1.call-start = ((), (), s32[]{:S(2)}) async-start(), calls=%async_computation.10 | async-start | bytes 2359296 | tf_op jit(solution)/shard_map/reduce_scatter | solution.py:273
  2416.0 369.4 %reduce-scatter.8.cloned.1.call-start = ((), (), s32[]{:S(2)}) async-start(), calls=%async_computation.11 | async-start | bytes 2359296 | tf_op jit(solution)/shard_map/reduce_scatter | solution.py:276
  2525.1 15.9 copy-start.44
  2546.6 240.6 %copy-start.1 = (bf16[2,256,2048]{2,1,0:T(8,128)(2,1)S(1)}, bf16[2,256,2048]{2,1,0:T(8,128)(2,1)}, u32[]{:S(2)}) copy-start(bf16[2,256,2048]{2,1,0:T(8,128)(2,1)} %param.33) | copy-start | bytes 6291460
  (73 other events, 244.5 us)
Sparse Core Ops, SparseCore 0:
  28.9 88.2 all-reduce.18
  2171.0 182.6 all-reduce.20
  2356.9 54.8 reduce-scatter.13
  2415.2 84.5 all-reduce.22
  2503.3 68.7 reduce-scatter.11
  2575.5 67.6 reduce-scatter.9
  2646.7 67.6 reduce-scatter.5
  2717.9 67.3 reduce-scatter.7
